TPU v7x, 32 devices: a whole 2x2x4 slice. The times are simulated.
32 devices in a mesh: groups: 2 (over x), ctx: 16 (over z, y, core).
Axes of the slice: x: 2, y: 2, z: 4, core: 2. Of those that a mesh axis runs over, the one named last changes fastest.
Arguments:
- hidden: bfloat16 [4096, 2048], P(('groups', 'ctx')), parts along dimension 0, may hold values from -6 to 6
- w_query: bfloat16 [2048, 2048], P('ctx')
- w_keyval: bfloat16 [2048, 1024], P('ctx')
- w_out: bfloat16 [2048, 2048], P('ctx'), may hold values from -1.796875 to 1.796875
- global_blocks: int32 [4], P('groups'), parts along dimension 0, may hold values from 0 to 15, as said below
- cotangent: bfloat16 [4096, 2048], P(('groups', 'ctx')), parts along dimension 0, may hold values from -6 to 6
Outputs:
- combined: bfloat16 [4096, 2048], P(('groups', 'ctx')), parts along dimension 0
- input_grad: bfloat16 [4096, 2048], P(('groups', 'ctx')), parts along dimension 0
There are 2 independent parts, one for each index of `groups`. A program takes and returns all parts, laid end to end along the dimension named above; an argument that names none is the same for every part. Nothing has to cross between parts.
Inputs may be any that keep to these rules, and one draw needn't show every extreme that they name: `global_blocks`: 2 distinct block indices; the last block, 15, is always one of them, at a position drawn from the seed.
All inputs are finite; a program needn't handle non-finite values.
Results may differ from a plain program's by a relative error of at most 0.0098.
Values may be sent and summed in bfloat16 or wider, within the bound.
No kernel may reach another device: no remote copies, remote signals or barrier semaphores. Data moves between devices by JAX's collectives and lax.ppermute only.
A program may use at most 128 MiB of HBM per device.

v0:
```python
import jax
import jax.numpy as jnp
from jax import lax
from jax.sharding import PartitionSpec as P

HEADS = 16
KVH = 4
HDIM = 128
BLK = 128
epsilon = 1e-05


def with_halo(cells, sides, width):
    for axis, dim in sides:
        count = lax.axis_size(axis)
        ends = count - 1
        head = lax.slice_in_dim(cells, 0, width, axis=dim)
        tail = lax.slice_in_dim(cells, cells.shape[dim] - width, cells.shape[dim], axis=dim)
        cells = jnp.concatenate(
            [
                lax.ppermute(tail, axis, [(i, (i + 1) % count) for i in range(ends)]),
                cells,
                lax.ppermute(head, axis, [((i + 1) % count, i) for i in range(ends)]),
            ],
            axis=dim,
        )
    return cells


def spread_2(value, axis, source):
    kept = jnp.where(lax.axis_index(axis) == source, value, 0).astype(value.dtype)
    return lax.psum(kept, axis)


def normalize(values):
    widened = values.astype(jnp.float32)
    inv_rms = lax.rsqrt(jnp.mean(widened * widened, axis=1, keepdims=True) + epsilon)
    return (widened * inv_rms, inv_rms)


def split_heads(row_values, block_count):
    return row_values.reshape(block_count, BLK, KVH, HEADS // KVH, HDIM)


def body(hidden, w_query, w_keyval, w_out, global_blocks, cotangent):
    row_count = hidden.shape[0]
    per_device = row_count // BLK
    block_count = 2 * per_device
    kv_width = w_keyval.shape[1]
    half_width = kv_width // 2
    global_count = global_blocks.shape[0]
    devices = lax.axis_size("ctx")
    my_index = lax.axis_index("ctx")
    full_query, full_keyval, full_output = (
        lax.all_gather(w_query, "ctx", axis=0, tiled=True),
        lax.all_gather(w_keyval, "ctx", axis=0, tiled=True),
        lax.all_gather(w_out, "ctx", axis=0, tiled=True),
    )
    stacked = jnp.concatenate([hidden, hidden[::-1, ::-1]], axis=0)
    scaled, inv_rms = normalize(stacked)
    normed = scaled.astype(jnp.bfloat16)
    queries = jnp.dot(normed, full_query, preferred_element_type=jnp.float32).astype(jnp.bfloat16)
    keyvals = jnp.dot(normed, full_keyval, preferred_element_type=jnp.float32).astype(jnp.bfloat16)
    kv_blocks = keyvals.reshape(2, per_device, BLK, kv_width)
    border = jnp.concatenate([kv_blocks[1, -1], kv_blocks[0, -1]], axis=0)
    padded = with_halo(border, (("ctx", 0),), BLK)
    neighbors = jnp.stack([padded[:BLK], padded[3 * BLK :]])
    extended = jnp.concatenate([neighbors[:, None], kv_blocks], axis=1)
    slot_index = global_blocks % per_device
    plain_owner = global_blocks // per_device
    owners = jnp.stack([plain_owner, devices - 1 - plain_owner])
    pieces = jnp.take(kv_blocks, slot_index, axis=1)
    collected = []
    for branch in range(2):
        for position in range(global_count):
            collected.append(spread_2(pieces[branch, position], "ctx", owners[branch, position]))
    global_keys = jnp.stack(collected).reshape(2, global_count, BLK, kv_width)
    paired = jnp.concatenate([extended[:, :-1], extended[:, 1:]], axis=2)
    spread = global_keys.reshape(2, 1, global_count * BLK, kv_width)
    key_sets = jnp.concatenate([paired, spread], axis=2).reshape(block_count, -1, kv_width)
    key_count = key_sets.shape[1]
    keys_only = key_sets[:, :, :half_width].reshape(block_count, key_count, KVH, HDIM)
    values_only = key_sets[:, :, half_width:].reshape(block_count, key_count, KVH, HDIM)
    first_ids = jnp.stack([my_index * per_device, (devices - 1 - my_index) * per_device])
    block_ids = (first_ids[:, None] + jnp.arange(per_device)[None, :]).reshape(block_count)
    global_flags = (global_blocks[None, :] != block_ids[:, None]) & (
        global_blocks[None, :] != block_ids[:, None] - 1
    )
    key_flags = jnp.concatenate(
        [(block_ids >= 1)[:, None], (block_ids >= 0)[:, None], global_flags], axis=1
    )
    validity = jnp.repeat(key_flags, BLK, axis=1)[:, None, None, None, :]
    query_heads = split_heads(queries, block_count)
    scores = jnp.einsum(
        "bqgrd,bkgd->bgrqk", query_heads, keys_only, preferred_element_type=jnp.float32
    ) * HDIM ** (-0.5)
    scores = jnp.where(validity, scores, -jnp.inf)
    exponent = jnp.exp(scores - jnp.max(scores, axis=-1, keepdims=True))
    prob_full = exponent / jnp.sum(exponent, axis=-1, keepdims=True)
    prob_half = prob_full.astype(jnp.bfloat16)
    attended = jnp.einsum(
        "bgrqk,bkgd->bqgrd", prob_half, values_only, preferred_element_type=jnp.float32
    )
    attended = attended.astype(jnp.bfloat16).reshape(2 * row_count, -1)
    outputs = jnp.dot(attended, full_output, preferred_element_type=jnp.float32)
    combined = (outputs[:row_count] + outputs[row_count:][::-1]).astype(jnp.bfloat16)
    grad_rows = jnp.concatenate([cotangent, cotangent[::-1]], axis=0)
    grad_att = jnp.dot(grad_rows, full_output.T, preferred_element_type=jnp.float32).astype(
        jnp.bfloat16
    )
    upstream = split_heads(grad_att, block_count)
    grad_prob = jnp.einsum(
        "bqgrd,bkgd->bgrqk", upstream, values_only, preferred_element_type=jnp.float32
    )
    center = jnp.sum(prob_full * grad_prob, axis=-1, keepdims=True)
    grad_score = (prob_full * (grad_prob - center) * HDIM ** (-0.5)).astype(jnp.bfloat16)
    grad_query = jnp.einsum(
        "bgrqk,bkgd->bqgrd", grad_score, keys_only, preferred_element_type=jnp.float32
    )
    grad_query = grad_query.astype(jnp.bfloat16).reshape(2 * row_count, -1)
    grad_keys = jnp.einsum(
        "bgrqk,bqgrd->bkgd", grad_score, query_heads, preferred_element_type=jnp.float32
    ).reshape(block_count, key_count, half_width)
    grad_values = jnp.einsum(
        "bgrqk,bqgrd->bkgd", prob_half, upstream, preferred_element_type=jnp.float32
    ).reshape(block_count, key_count, half_width)
    key_terms = jnp.concatenate([grad_keys, grad_values], axis=-1).reshape(
        2, per_device, 2 + global_count, BLK, kv_width
    )
    ext_grad = jnp.pad(key_terms[:, :, 0], ((0, 0), (0, 1), (0, 0), (0, 0))) + jnp.pad(
        key_terms[:, :, 1], ((0, 0), (1, 0), (0, 0), (0, 0))
    )
    outgoing = jnp.concatenate([ext_grad[0, 0], ext_grad[1, 0]], axis=0)
    returned = with_halo(outgoing.astype(jnp.bfloat16), (("ctx", 0),), BLK).astype(outgoing.dtype)
    own_grads = ext_grad[:, 1:]
    own_grads = own_grads.at[0, -1].add(returned[3 * BLK :])
    own_grads = own_grads.at[1, -1].add(returned[:BLK])
    totals = lax.psum(jnp.sum(key_terms[:, :, 2:], axis=1), "ctx")
    hot_table = (
        (jnp.arange(per_device)[None, None, :] == slot_index[None, :, None])
        & (owners[:, :, None] == my_index)
    ).astype(jnp.float32)
    own_grads = own_grads + jnp.sum(hot_table[:, :, :, None, None] * totals[:, :, None], axis=1)
    key_grads = own_grads.reshape(2 * row_count, kv_width).astype(jnp.bfloat16)
    grad_norm = jnp.dot(grad_query, full_query.T, preferred_element_type=jnp.float32)
    grad_norm = grad_norm + jnp.dot(key_grads, full_keyval.T, preferred_element_type=jnp.float32)
    grad_in = inv_rms * (grad_norm - scaled * jnp.mean(grad_norm * scaled, axis=1, keepdims=True))
    input_grad = (grad_in[:row_count] + grad_in[row_count:][::-1, ::-1]).astype(jnp.bfloat16)
    return (combined, input_grad)


def solution(mesh):
    return jax.shard_map(
        body,
        mesh=mesh,
        in_specs=(
            P(("groups", "ctx"), None),
            P("ctx", None),
            P("ctx", None),
            P("ctx", None),
            P("groups"),
            P(("groups", "ctx"), None),
        ),
        out_specs=(P(("groups", "ctx"), None), P(("groups", "ctx"), None)),
        check_vma=False,
    )
```

profile of v0, /device:TPU:0, one launch (start us, length us, event | category | flops | bytes accessed | tf_op | source)
XLA Modules:
  0.0 514.8 jit_solution(2713949893909427027)
XLA Ops:
  7.9 7.0 %rev.12 = bf16[128,2048]{1,0:T(8,128)(2,1)S(1)} reverse(bf16[128,2048]{1,0:T(8,128)(2,1)} %param.10), dimensions={0,1} | reverse | bytes 1048576 | tf_op jit(solution)/shard_map/rev | solution.py:59
  14.9 1.4 fusion.65
  20.4 1.3 fusion.21
  21.7 41.7 %all-gather.4.cloned.1.call-done = bf16[2048,1024]{1,0:T(8,128)(2,1)} async-done(((bf16[128,1024]{1,0:T(8,128)(2,1)}), bf16[2048,1024]{1,0:T(8,128)(2,1)}) %all-gather.4.cloned.1.call-update) | async-done | bytes 4194320 | tf_op jit(solution)/shard_map/all_gather | solution.py:56
  63.5 3.6 convolution_convert_fusion.2
  67.1 1.0 fusion.64
  69.8 1.3 collective-permute-start.1
  71.1 3.0 collective-permute-start
  74.2 5.2 %rev.14 = bf16[128,2048]{1,0:T(8,128)(2,1)} reverse(bf16[128,2048]{1,0:T(8,128)(2,1)S(1)} %copy-done.12), dimensions={0} | reverse | bytes 1048576 | tf_op jit(solution)/shard_map/rev | solution.py:107
  81.5 79.1 %all-reduce.8.cloned.1.call-done = (bf16[1,128,1024]{2,1,0:T(8,128)(2,1)}, bf16[1,128,1024]{2,1,0:T(8,128)(2,1)}, bf16[1,128,1024]{2,1,0:T(8,128)(2,1)}, bf16[1,128,1024]{2,1,0:T(8,128)(2,1)}) async-done(((bf16[1,128,1024]{2,1,0:T(8,128)(2,1)}, bf16[1,128,1024]{2,1,0:T(8,128)(2,1)}, bf16[1,128,1024]{2,1,0:T(8,128)(2,1)}, bf16[1,128,1024]{2,1,0:T(8,128)(2,1)}), (bf16[1,128,1024]{2,1,0:T(8,128)(2,1)}, ...) | async-done | bytes 1048592 | tf_op jit(solution)/shard_map/psum | solution.py:32
  160.7 1.3 pad_maximum_fusion.2
  162.5 1.4 maximum_bitcast_fusion
  164.0 1.1 fusion.63
  165.1 72.0 %all-gather.6.cloned.1.call-done = bf16[2048,2048]{1,0:T(8,128)(2,1)} async-done(((bf16[128,2048]{1,0:T(8,128)(2,1)}), bf16[2048,2048]{1,0:T(8,128)(2,1)}) %all-gather.6.cloned.1.call-update) | async-done | bytes 8388624 | tf_op jit(solution)/shard_map/all_gather | solution.py:55
  237.2 5.8 %convolution_convert_fusion.1 = bf16[256,2048]{1,0:T(8,128)(2,1)S(1)} fusion(bf16[2048,2048]{1,0:T(8,128)(2,1)} %all-gather.6.cloned.1.call-done, f32[256]{0:T(256)S(1)} %add_rsqrt_fusion, bf16[128,2048]{1,0:T(8,128)(2,1)S(1)} %rev.12, bf16[128,2048]{1,0:T(8,128)(2,1)S(1)} %copy-done.2), kind=kOutput, calls=%fused_computation.31 | convolution fusion | flops 2151153664 | bytes 10486784 | tf_op jit(solution)/shard_map/dot_general | solution.py:62
  243.7 1.7 copy.34
  245.4 67.0 %all-gather.8.cloned.1.call-done = bf16[2048,2048]{1,0:T(8,128)(2,1)} async-done(((bf16[128,2048]{1,0:T(8,128)(2,1)}), bf16[2048,2048]{1,0:T(8,128)(2,1)}) %all-gather.8.cloned.1.call-update) | async-done | bytes 8388624 | tf_op jit(solution)/shard_map/all_gather | solution.py:57
  312.3 6.1 %convolution_convert_fusion = bf16[256,2048]{1,0:T(8,128)(2,1)S(1)} fusion(bf16[2048,2048]{1,0:T(8,128)(2,1)} %all-gather.8.cloned.1.call-done, bf16[128,2048]{1,0:T(8,128)(2,1)} %rev.14, bf16[128,2048]{1,0:T(8,128)(2,1)} %param.15), kind=kOutput, calls=%fused_computation.30 | convolution fusion | flops 2150105088 | bytes 10485760 | tf_op jit(solution)/shard_map/dot_general | solution.py:108
  319.2 1.2 copy.36
  320.4 4.5 fusion.69
  324.9 7.5 %fusion.67 = (f32[2,4,4,128]{3,2,1,0:T(4,128)S(1)}, f32[2,4,4,128,512]{3,4,2,1,0:T(8,128)}) fusion(pred[2,512]{1,0:T(4,128)(4,1)S(1)} %bitcast.176, bf16[2,512,4,128,1]{1,3,4,2,0:T(8,128)(2,1)} %bitcast.170, bf16[2,128,4,4,128]{1,4,3,2,0:T(8,128)(2,1)S(1)} %copy-done.10), kind=kOutput, calls=%fused_computation.108 | convolution fusion | flops 545260032 | bytes 10503168 | tf_op jit(solution)/shard_map/sub | solution.py:98
  332.4 5.3 %fusion.37 = bf16[2,128,4,4,128]{1,4,3,2,0:T(8,128)(2,1)} fusion(bf16[2,512,4,128,1]{1,3,4,2,0:T(8,128)(2,1)S(1)} %bitcast.166, f32[2,4,4,128,512]{3,4,2,1,0:T(8,128)} %get-tuple-element.49, f32[2,4,4,128]{3,2,1,0:T(4,128)S(1)} %get-tuple-element.48), kind=kOutput, calls=%fused_computation.50 | convolution fusion | flops 541589504 | bytes 10502144 | tf_op jit(solution)/shard_map/bgrqk,bkgd->bqgrd/dot_general | solution.py:101
  338.6 1.5 fusion.28
  340.1 14.6 %fusion.36 = bf16[2,128,4,4,128]{1,4,3,2,0:T(8,128)(2,1)} fusion(bf16[2,512,4,128,1]{1,3,4,2,0:T(8,128)(2,1)} %bitcast.171, f32[2,4,512,128,4]{3,2,4,1,0:T(8,128)} %fusion.69, f32[2,4,4,128,512]{3,4,2,1,0:T(8,128)} %get-tuple-element.49, f32[2,4,4,128]{3,2,1,0:T(4,128)S(1)} %get-tuple-element.48), kind=kOutput, calls=%fused_computation.49 | convolution fusion | flops 552079872 | bytes 18890752 | tf_op jit(solution)/shard_map/bgrqk,bkgd->bqgrd/dot_general | solution.py:117
  354.6 13.4 %fusion.31 = f32[2,512,4,128]{1,3,2,0:T(8,128)} fusion(bf16[2,128,4,4,128]{1,4,3,2,0:T(8,128)(2,1)S(1)} %copy-done.11, f32[2,4,512,128,4]{3,2,4,1,0:T(8,128)} %fusion.69, f32[2,4,4,128,512]{3,4,2,1,0:T(8,128)} %get-tuple-element.49, f32[2,4,4,128]{3,2,1,0:T(4,128)S(1)} %get-tuple-element.48), kind=kOutput, calls=%fused_computation.46 | convolution fusion | flops 551555584 | bytes 19939328 | tf_op jit(solution)/shard_map/bgrqk,bqgrd->bkgd/dot_general | solution.py:121
  368.1 1.7 concatenate.59
  369.8 1.9 copy.39
  371.7 2.9 concatenate.58
  374.6 2.9 copy.38
  377.5 2.5 maximum_bitcast_fusion.2
  380.0 1.5 fusion.23
  381.5 2.0 copy.29
  383.5 1.9 reshape.285
  385.4 1.9 copy.33
  387.3 1.6 reshape.287
  389.8 1.3 collective-permute-start.3
  391.1 3.7 collective-permute-start.2
  394.9 5.8 %fusion.68 = f32[256,2048]{1,0:T(8,128)S(1)} fusion(bf16[256,2048]{1,0:T(8,128)(2,1)S(1)} %copy-done.8, bf16[2048,2048]{1,0:T(8,128)(2,1)} %all-gather.8.cloned.1.call-done), kind=kOutput, calls=%fused_computation.109 | convolution fusion | flops 2147483648 | bytes 11534336 | tf_op jit(solution)/shard_map/dot_general | solution.py:105
  400.7 7.9 %fusion.70 = f32[256,2048]{1,0:T(8,128)} fusion(bf16[256,2048]{1,0:T(8,128)(2,1)S(1)} %copy-done.9, bf16[2048,2048]{1,0:T(8,128)(2,1)} %all-gather.6.cloned.1.call-done), kind=kOutput, calls=%fused_computation.111 | convolution fusion | flops 2147483648 | bytes 11534336 | tf_op jit(solution)/shard_map/dot_general | solution.py:145
  408.6 1.1 slice.178
  409.7 6.8 %rev.13 = f32[128,2048]{1,0:T(8,128)S(1)} reverse(f32[128,2048]{1,0:T(8,128)} %slice.178), dimensions={0} | reverse | bytes 2097152 | tf_op jit(solution)/shard_map/rev | solution.py:106
  416.6 2.1 fusion.42
  420.0 1.1 fusion.53
  421.1 71.3 %all-reduce.6.cloned.1.call-done = f32[2,2,128,1024]{3,2,0,1:T(8,128)} async-done(((f32[2,2,128,1024]{3,2,0,1:T(8,128)}), f32[2,2,128,1024]{3,2,0,1:T(8,128)}) %all-reduce.6.cloned.1.call-update) | async-done | bytes 2097168 | tf_op jit(solution)/shard_map/psum | solution.py:138
  492.4 2.2 multiply_reduce_fusion
  495.2 3.1 fusion.18
  498.8 1.1 slice.187
  499.8 7.5 %rev.15 = f32[128,2048]{1,0:T(8,128)S(1)} reverse(f32[128,2048]{1,0:T(8,128)} %slice.187), dimensions={0,1} | reverse | bytes 2097152 | tf_op jit(solution)/shard_map/rev | solution.py:148
  (70 shorter events, 12.9 us)
Async XLA Ops:
  7.2 56.3 %all-gather.4.cloned.1.call-start = ((), (), s32[]{:S(2)}) async-start(), calls=%async_computation | async-start | bytes 4456448 | tf_op jit(solution)/shard_map/all_gather | solution.py:56
  7.9 152.8 %all-reduce.8.cloned.1.call-start = ((), (), s32[]{:S(2)}) async-start(), calls=%async_computation.4 | async-start | bytes 2097152 | tf_op jit(solution)/shard_map/psum | solution.py:32
  14.9 222.2 %copy-start.4 = (bf16[128,2048]{1,0:T(8,128)(2,1)}, bf16[128,2048]{1,0:T(8,128)(2,1)S(1)}, u32[]{:S(2)}) copy-start(bf16[128,2048]{1,0:T(8,128)(2,1)S(1)} %rev.12) | copy-start | bytes 1572868
  21.7 47.9 %copy-start.13 = (s32[2]{0:T(128)S(1)}, s32[2]{0:T(128)}, u32[]{:S(2)}) copy-start(s32[2]{0:T(128)} %param.14) | copy-start | bytes 28
  21.7 52.5 %copy-start.12 = (bf16[128,2048]{1,0:T(8,128)(2,1)S(1)}, bf16[128,2048]{1,0:T(8,128)(2,1)}, u32[]{:S(2)}) copy-start(bf16[128,2048]{1,0:T(8,128)(2,1)} %param.15) | copy-start | bytes 1572868
  68.2 169.0 %all-gather.6.cloned.1.call-start = ((), (), s32[]{:S(2)}) async-start(), calls=%async_computation.1 | async-start | bytes 8912896 | tf_op jit(solution)/shard_map/all_gather | solution.py:55
  68.9 243.4 %all-gather.8.cloned.1.call-start = ((), (), s32[]{:S(2)}) async-start(), calls=%async_computation.2 | async-start | bytes 8912896 | tf_op jit(solution)/shard_map/all_gather | solution.py:57
  69.5 422.9 %all-reduce.6.cloned.1.call-start = ((), (), s32[]{:S(2)}) async-start(), calls=%async_computation.3 | async-start | bytes 4194304 | tf_op jit(solution)/shard_map/psum | solution.py:138
  69.8 10.7 %collective-permute-start.1 = (bf16[128,1024]{1,0:T(8,128)(2,1)S(1)}, bf16[128,1024]{1,0:T(8,128)(2,1)S(1)}, u32[]{:S(2)}, u32[]{:S(2)}) collective-permute-start(bf16[128,1024]{1,0:T(8,128)(2,1)S(1)} %get-tuple-element.43), channel_id=1, source_target_pairs={{1,0},{2,1},{3,2},{4,3},{5,4},{6,5},{7,6},{8,7},{9,8},{10,9},{11,1... | collective-permute-start | bytes 786440 | tf_op jit(solution)/shard_map/ppermute | solution.py:23
  71.1 9.4 %collective-permute-start = (bf16[128,1024]{1,0:T(8,128)(2,1)S(1)}, bf16[128,1024]{1,0:T(8,128)(2,1)S(1)}, u32[]{:S(2)}, u32[]{:S(2)}) collective-permute-start(bf16[128,1024]{1,0:T(8,128)(2,1)S(1)} %get-tuple-element.38), channel_id=1, source_target_pairs={{0,1},{1,2},{2,3},{3,4},{4,5},{5,6},{6,7},{7,8},{8,9},{9,10},{10,1... | collective-permute-start | bytes 786440 | tf_op jit(solution)/shard_map/ppermute | solution.py:21
  162.5 74.6 %copy-start.2 = (bf16[128,2048]{1,0:T(8,128)(2,1)S(1)}, bf16[128,2048]{1,0:T(8,128)(2,1)}, u32[]{:S(2)}) copy-start(bf16[128,2048]{1,0:T(8,128)(2,1)} %param.10) | copy-start | bytes 1572868
  320.4 4.5 copy-start.10
  332.4 6.1 %copy-start.14 = (f32[2,4,4,128,512]{3,4,2,1,0:T(8,128)S(1)}, f32[2,4,4,128,512]{3,4,2,1,0:T(8,128)}, u32[]{:S(2)}) copy-start(f32[2,4,4,128,512]{3,4,2,1,0:T(8,128)} %get-tuple-element.49) | copy-start | bytes 25165828
  340.1 14.6 %copy-start.11 = (bf16[2,128,4,4,128]{1,4,3,2,0:T(8,128)(2,1)S(1)}, bf16[2,128,4,4,128]{1,4,3,2,0:T(8,128)(2,1)}, u32[]{:S(2)}) copy-start(bf16[2,128,4,4,128]{1,4,3,2,0:T(8,128)(2,1)} %copy.34) | copy-start | bytes 3145732
  377.5 2.5 copy-start
  381.5 7.4 %copy-start.1 = (f32[2,1,128,1024]{3,2,1,0:T(8,128)S(1)}, f32[2,1,128,1024]{3,2,1,0:T(8,128)}, u32[]{:S(2)}) copy-start(f32[2,1,128,1024]{3,2,1,0:T(8,128)} %get-tuple-element.33) | copy-start | bytes 3145732
  388.9 5.9 %copy-start.8 = (bf16[256,2048]{1,0:T(8,128)(2,1)S(1)}, bf16[256,2048]{1,0:T(8,128)(2,1)}, u32[]{:S(2)}) copy-start(bf16[256,2048]{1,0:T(8,128)(2,1)} %reshape.285) | copy-start | bytes 3145732
  389.8 29.0 %collective-permute-start.3 = (bf16[128,1024]{1,0:T(8,128)(2,1)}, bf16[128,1024]{1,0:T(8,128)(2,1)}, u32[]{:S(2)}, u32[]{:S(2)}) collective-permute-start(bf16[128,1024]{1,0:T(8,128)(2,1)} %get-tuple-element.37), channel_id=1, source_target_pairs={{1,0},{2,1},{3,2},{4,3},{5,4},{6,5},{7,6},{8,7},{9,8},{10,9},{11,1... | collective-permute-start | bytes 786440 | tf_op jit(solution)/shard_map/ppermute | solution.py:23
  391.1 27.7 %collective-permute-start.2 = (bf16[128,1024]{1,0:T(8,128)(2,1)S(1)}, bf16[128,1024]{1,0:T(8,128)(2,1)}, u32[]{:S(2)}, u32[]{:S(2)}) collective-permute-start(bf16[128,1024]{1,0:T(8,128)(2,1)S(1)} %get-tuple-element.36), channel_id=1, source_target_pairs={{0,1},{1,2},{2,3},{3,4},{4,5},{5,6},{6,7},{7,8},{8,9},{9,10},{10,1... | collective-permute-start | bytes 786440 | tf_op jit(solution)/shard_map/ppermute | solution.py:21
  394.9 5.8 %copy-start.9 = (bf16[256,2048]{1,0:T(8,128)(2,1)S(1)}, bf16[256,2048]{1,0:T(8,128)(2,1)}, u32[]{:S(2)}) copy-start(bf16[256,2048]{1,0:T(8,128)(2,1)} %reshape.287) | copy-start | bytes 3145732
  400.7 7.9 %copy-start.7 = (f32[256,2048]{1,0:T(8,128)}, f32[256,2048]{1,0:T(8,128)S(1)}, u32[]{:S(2)}) copy-start(f32[256,2048]{1,0:T(8,128)S(1)} %fusion.68) | copy-start | bytes 6291460
  420.0 74.8 %copy-start.3 = (bf16[128,2048]{1,0:T(8,128)(2,1)S(1)}, bf16[128,2048]{1,0:T(8,128)(2,1)}, u32[]{:S(2)}) copy-start(bf16[128,2048]{1,0:T(8,128)(2,1)} %param.10) | copy-start | bytes 1572868
  420.0 74.8 %copy-start.5 = (bf16[128,2048]{1,0:T(8,128)(2,1)S(1)}, bf16[128,2048]{1,0:T(8,128)(2,1)}, u32[]{:S(2)}) copy-start(bf16[128,2048]{1,0:T(8,128)(2,1)} %copy-done.4) | copy-start | bytes 1572868
  492.4 2.8 copy-start.6
Sparse Core Ops, SparseCore 0:
  10.2 53.2 all-gather.3
  68.3 92.3 all-reduce.7
  162.8 74.2 all-gather.5
  239.2 73.1 all-gather.7
  395.0 97.3 all-reduce.5
where the time goes:
time: 517 us; the launch traced here: 515 us
  waiting for transfers between devices  333 us (64%)
  matrix products  79.2 us (15%)
  local copies, waits for them, and re-layouts  57.9 us (11%)
  other arithmetic  18.3 us (4%)
  between operations  16.8 us (3%)
  starting transfers between devices  9.53 us (2%)
    psum x1, waiting for transfers between devices, spread_2(): return lax.psum(kept, axis)  79.1 us
    all_gather x1, waiting for transfers between devices, body(): lax.all_gather(w_query, 'ctx', axis=0, tiled=True)  72 us
    psum x1, waiting for transfers between devices, body(): totals = lax.psum(jnp.sum(key_terms[:, :, 2:], axis=1), 'ctx')  71.3 us
    all_gather x1, waiting for transfers between devices, body(): lax.all_gather(w_out, 'ctx', axis=0, tiled=True)  67 us
    all_gather x1, waiting for transfers between devices, body(): lax.all_gather(w_keyval, 'ctx', axis=0, tiled=True)  41.7 us
    dot_general x1, matrix products, body(): jnp.einsum('bgrqk,bkgd->bqgrd', grad_score, keys_only, preferred_element_...  14.6 us
    dot_general x1, matrix products, body(): jnp.einsum('bgrqk,bqgrd->bkgd', grad_score, query_heads, preferred_elemen...  13.4 us
  transfers between devices with their start and end apart: 9, of which 5 were waited for; matrix products, arithmetic and copies ran while one was open for 11% of the time, Pallas kernels for 0%

commit v1 on v0

--- a/solution.py
+++ b/solution.py
@@ -2,6 +2,7 @@
 import jax.numpy as jnp
 from jax import lax
 from jax.sharding import PartitionSpec as P
+from jax.lax import all_gather
 
 HEADS = 16
 KVH = 4
@@ -135,7 +136,9 @@
     own_grads = ext_grad[:, 1:]
     own_grads = own_grads.at[0, -1].add(returned[3 * BLK :])
     own_grads = own_grads.at[1, -1].add(returned[:BLK])
-    totals = lax.psum(jnp.sum(key_terms[:, :, 2:], axis=1), "ctx")
+    point = jnp.sum(key_terms[:, :, 2:], axis=1)
+    spare = all_gather(point, "ctx")
+    totals = jnp.sum(spare, 0)
     hot_table = (
         (jnp.arange(per_device)[None, None, :] == slot_index[None, :, None])
         & (owners[:, :, None] == my_index)

time: 517 us -> 576 us (1.11)
  waiting for transfers between devices: 333 us -> 364 us
  local copies, waits for them, and re-layouts: 57.9 us -> 67.7 us
  other arithmetic: 18.3 us -> 27.7 us
  matrix products: 79.2 us -> 86.8 us
    all_gather x0 -> x1, waiting for transfers between devices: none -> 104 us  [body(): spare = all_gather(point, 'ctx')]
    psum x1 -> x0, waiting for transfers between devices: 71.3 us -> none  [body(): totals = lax.psum(jnp.sum(key_terms[:, :, 2:], axis=1), 'ctx')]
    reduce_sum x1, other arithmetic: 1.5 us -> 12.1 us  [body(): totals = jnp.sum(spare, 0)]
  transfers between devices with their start and end apart: 9 -> 9, of which waited for: 5 -> 5; matrix products, arithmetic and copies ran while one was open for 11% -> 16% of each run, Pallas kernels for 0% -> 0%
where the time goes in v1:
time: 576 us; the launch traced here: 572 us
  waiting for transfers between devices  364 us (63%)
  matrix products  86.8 us (15%)
  local copies, waits for them, and re-layouts  67.7 us (12%)
  other arithmetic  27.7 us (5%)
  between operations  16.7 us (3%)
  starting transfers between devices  9.34 us (2%)
    all_gather x1, waiting for transfers between devices, body(): spare = all_gather(point, 'ctx')  104 us
    psum x1, waiting for transfers between devices, spread_2(): return lax.psum(kept, axis)  79.1 us
    all_gather x1, waiting for transfers between devices, body(): lax.all_gather(w_query, 'ctx', axis=0, tiled=True)  72 us
    all_gather x1, waiting for transfers between devices, body(): lax.all_gather(w_out, 'ctx', axis=0, tiled=True)  64.9 us
    all_gather x1, waiting for transfers between devices, body(): lax.all_gather(w_keyval, 'ctx', axis=0, tiled=True)  42 us
    dot_general x1, matrix products, body(): jnp.einsum('bgrqk,bkgd->bqgrd', grad_score, keys_only, preferred_element_...  15.1 us
    dot_general x1, matrix products, body(): jnp.einsum('bgrqk,bqgrd->bkgd', grad_score, query_heads, preferred_elemen...  14.8 us
    reduce_sum x1, other arithmetic, body(): totals = jnp.sum(spare, 0)  12.1 us
  transfers between devices with their start and end apart: 9, of which 5 were waited for; matrix products, arithmetic and copies ran while one was open for 16% of the time, Pallas kernels for 0%

profile of v1, /device:TPU:0, one launch (start us, length us, event | category | flops | bytes accessed | tf_op | source)
XLA Modules:
  0.0 572.0 jit_solution(10216869749436170754)
XLA Ops:
  7.9 7.0 %rev.12 = bf16[128,2048]{1,0:T(8,128)(2,1)S(1)} reverse(bf16[128,2048]{1,0:T(8,128)(2,1)} %param.10), dimensions={0,1} | reverse | bytes 1048576 | tf_op jit(solution)/shard_map/rev | solution.py:60
  14.9 1.3 fusion.64
  20.1 1.4 fusion.21
  21.5 42.0 %all-gather.6.cloned.1.call-done = bf16[2048,1024]{1,0:T(8,128)(2,1)} async-done(((bf16[128,1024]{1,0:T(8,128)(2,1)}), bf16[2048,1024]{1,0:T(8,128)(2,1)}) %all-gather.6.cloned.1.call-update) | async-done | bytes 4194320 | tf_op jit(solution)/shard_map/all_gather | solution.py:57
  63.5 3.6 convolution_convert_fusion.2
  69.7 1.3 collective-permute-start.1
  71.0 3.0 collective-permute-start
  74.2 5.2 rev.14
  81.5 79.1 %all-reduce.5.cloned.1.call-done = (bf16[1,128,1024]{2,1,0:T(8,128)(2,1)}, bf16[1,128,1024]{2,1,0:T(8,128)(2,1)}, bf16[1,128,1024]{2,1,0:T(8,128)(2,1)}, bf16[1,128,1024]{2,1,0:T(8,128)(2,1)}) async-done(((bf16[1,128,1024]{2,1,0:T(8,128)(2,1)}, bf16[1,128,1024]{2,1,0:T(8,128)(2,1)}, bf16[1,128,1024]{2,1,0:T(8,128)(2,1)}, bf16[1,128,1024]{2,1,0:T(8,128)(2,1)}), (bf16[1,128,1024]{2,1,0:T(8,128)(2,1)}, ...) | async-done | bytes 1048592 | tf_op jit(solution)/shard_map/psum | solution.py:33
  160.6 1.3 pad_maximum_fusion.2
  162.5 1.4 maximum_bitcast_fusion
  163.9 1.2 fusion.62
  165.1 72.0 %all-gather.8.cloned.1.call-done = bf16[2048,2048]{1,0:T(8,128)(2,1)} async-done(((bf16[128,2048]{1,0:T(8,128)(2,1)}), bf16[2048,2048]{1,0:T(8,128)(2,1)}) %all-gather.8.cloned.1.call-update) | async-done | bytes 8388624 | tf_op jit(solution)/shard_map/all_gather | solution.py:56
  237.1 6.7 %convolution_convert_fusion.1 = bf16[256,2048]{1,0:T(8,128)(2,1)} fusion(bf16[2048,2048]{1,0:T(8,128)(2,1)} %all-gather.8.cloned.1.call-done, f32[256]{0:T(256)S(1)} %add_rsqrt_fusion, bf16[128,2048]{1,0:T(8,128)(2,1)S(1)} %rev.12, bf16[128,2048]{1,0:T(8,128)(2,1)S(1)} %copy-done), kind=kOutput, calls=%fused_computation.31 | convolution fusion | flops 2151153664 | bytes 10486784 | tf_op jit(solution)/shard_map/dot_general | solution.py:63
  243.8 1.8 reshape.286
  245.6 1.7 copy.54
  247.3 64.9 %all-gather.10.cloned.1.call-done = bf16[2048,2048]{1,0:T(8,128)(2,1)} async-done(((bf16[128,2048]{1,0:T(8,128)(2,1)}), bf16[2048,2048]{1,0:T(8,128)(2,1)}) %all-gather.10.cloned.1.call-update) | async-done | bytes 8388624 | tf_op jit(solution)/shard_map/all_gather | solution.py:58
  312.3 6.1 %convolution_convert_fusion = bf16[256,2048]{1,0:T(8,128)(2,1)S(1)} fusion(bf16[2048,2048]{1,0:T(8,128)(2,1)} %all-gather.10.cloned.1.call-done, bf16[128,2048]{1,0:T(8,128)(2,1)} %rev.14, bf16[128,2048]{1,0:T(8,128)(2,1)} %param.15), kind=kOutput, calls=%fused_computation.30 | convolution fusion | flops 2150105088 | bytes 10485760 | tf_op jit(solution)/shard_map/dot_general | solution.py:109
  318.4 1.6 reshape.288
  319.9 1.9 copy.56
  321.9 4.5 fusion.68
  326.4 7.8 %fusion.66 = (f32[2,4,4,128]{3,2,1,0:T(4,128)S(1)}, f32[2,4,4,128,512]{3,4,2,1,0:T(8,128)}) fusion(pred[2,512]{1,0:T(4,128)(4,1)S(1)} %bitcast.176, bf16[2,512,4,128,1]{1,3,4,2,0:T(8,128)(2,1)} %bitcast.170, bf16[2,128,4,4,128]{1,4,3,2,0:T(8,128)(2,1)} %copy.54), kind=kOutput, calls=%fused_computation.107 | convolution fusion | flops 545260032 | bytes 10503168 | tf_op jit(solution)/shard_map/sub | solution.py:99
  334.2 6.2 %fusion.27 = f32[2,512,4,128]{1,3,2,0:T(8,128)} fusion(bf16[2,128,4,4,128]{1,4,3,2,0:T(8,128)(2,1)S(1)} %copy.56, f32[2,4,4,128,512]{3,4,2,1,0:T(8,128)} %get-tuple-element.49, f32[2,4,4,128]{3,2,1,0:T(4,128)S(1)} %get-tuple-element.48), kind=kOutput, calls=%fused_computation.44 | convolution fusion | flops 541065216 | bytes 11550720 | tf_op jit(solution)/shard_map/bgrqk,bqgrd->bkgd/dot_general | solution.py:125
  340.4 2.9 concatenate.59
  343.3 1.9 copy.59
  345.2 14.8 %fusion.30 = f32[2,512,4,128]{1,3,2,0:T(8,128)} fusion(bf16[2,128,4,4,128]{1,4,3,2,0:T(8,128)(2,1)} %copy.54, f32[2,4,512,128,4]{3,2,4,1,0:T(8,128)} %fusion.68, f32[2,4,4,128,512]{3,4,2,1,0:T(8,128)} %get-tuple-element.49, f32[2,4,4,128]{3,2,1,0:T(4,128)S(1)} %get-tuple-element.48), kind=kOutput, calls=%fused_computation.45 | convolution fusion | flops 551555584 | bytes 19939328 | tf_op jit(solution)/shard_map/bgrqk,bqgrd->bkgd/dot_general | solution.py:122
  360.0 2.9 concatenate.58
  362.9 2.9 copy.58
  365.8 2.7 pad_maximum_fusion
  368.7 5.5 fusion.36
  374.1 2.7 copy.49
  376.8 2.6 reshape.287
  379.4 6.3 %fusion.67 = f32[256,2048]{1,0:T(8,128)S(1)} fusion(bf16[256,2048]{1,0:T(8,128)(2,1)} %reshape.287, bf16[2048,2048]{1,0:T(8,128)(2,1)} %all-gather.10.cloned.1.call-done), kind=kOutput, calls=%fused_computation.108 | convolution fusion | flops 2147483648 | bytes 11534336 | tf_op jit(solution)/shard_map/dot_general | solution.py:106
  385.7 1.4 copy-done.4
  388.1 8.9 %rev.13 = f32[128,2048]{1,0:T(8,128)} reverse(f32[128,2048]{1,0:T(8,128)} %slice.178), dimensions={0} | reverse | bytes 2097152 | tf_op jit(solution)/shard_map/rev | solution.py:107
  397.0 15.1 %fusion.35 = bf16[2,128,4,4,128]{1,4,3,2,0:T(8,128)(2,1)} fusion(bf16[2,512,4,128,1]{1,3,4,2,0:T(8,128)(2,1)} %bitcast.171, f32[2,4,512,128,4]{3,2,4,1,0:T(8,128)} %fusion.68, f32[2,4,4,128,512]{3,4,2,1,0:T(8,128)} %get-tuple-element.49, f32[2,4,4,128]{3,2,1,0:T(4,128)S(1)} %get-tuple-element.48), kind=kOutput, calls=%fused_computation.48 | convolution fusion | flops 552079872 | bytes 18890752 | tf_op jit(solution)/shard_map/bgrqk,bkgd->bqgrd/dot_general | solution.py:118
  412.1 2.6 copy.53
  414.8 2.6 reshape.289
  417.4 1.5 maximum_bitcast_fusion.2
  419.1 1.3 collective-permute-start.3
  420.4 3.5 collective-permute-start.2
  423.9 7.1 %fusion.69 = f32[256,2048]{1,0:T(8,128)} fusion(bf16[256,2048]{1,0:T(8,128)(2,1)S(1)} %copy-done.6, bf16[2048,2048]{1,0:T(8,128)(2,1)} %all-gather.8.cloned.1.call-done), kind=kOutput, calls=%fused_computation.110 | convolution fusion | flops 2147483648 | bytes 11534336 | tf_op jit(solution)/shard_map/dot_general | solution.py:148
  434.0 103.9 %all-gather.12.cloned.1.call-done = f32[32,1,2,128,1024]{4,3,0,2,1:T(8,128)} async-done(((f32[2,1,2,128,1024]{4,3,0,2,1:T(8,128)}), f32[32,1,2,128,1024]{4,3,0,2,1:T(8,128)}) %all-gather.12.cloned.1.call-update) | async-done | bytes 33554448 | tf_op jit(solution)/shard_map/all_gather | solution.py:140
  537.8 12.1 %reduce_sum.63 = f32[2,2,128,1024]{3,2,0,1:T(8,128)S(1)} reduce(f32[16,2,2,128,1024]{4,3,1,0,2:T(8,128)} %bitcast.163, f32[]{:T(128)} %constant.114.clone.1), dimensions={0}, to_apply=%region_8.9 | reduce | flops 7864320 | bytes 35651588 | tf_op jit(solution)/shard_map/reduce_sum | solution.py:141
  550.3 1.5 fusion.45
  552.5 3.1 fusion.18
  556.0 1.0 slice.187
  557.1 7.5 %rev.15 = f32[128,2048]{1,0:T(8,128)S(1)} reverse(f32[128,2048]{1,0:T(8,128)} %slice.187), dimensions={0,1} | reverse | bytes 2097152 | tf_op jit(solution)/shard_map/rev | solution.py:151
  (59 shorter events, 13.9 us)
Async XLA Ops:
  7.2 56.3 %all-gather.6.cloned.1.call-start = ((), (), s32[]{:S(2)}) async-start(), calls=%async_computation | async-start | bytes 4456448 | tf_op jit(solution)/shard_map/all_gather | solution.py:57
  7.9 152.7 %all-reduce.5.cloned.1.call-start = ((), (), s32[]{:S(2)}) async-start(), calls=%async_computation.4 | async-start | bytes 2097152 | tf_op jit(solution)/shard_map/psum | solution.py:33
  21.5 48.2 %copy-start.8 = (s32[2]{0:T(128)S(1)}, s32[2]{0:T(128)}, u32[]{:S(2)}) copy-start(s32[2]{0:T(128)} %param.14) | copy-start | bytes 28
  21.5 52.7 %copy-start.7 = (bf16[128,2048]{1,0:T(8,128)(2,1)S(1)}, bf16[128,2048]{1,0:T(8,128)(2,1)}, u32[]{:S(2)}) copy-start(bf16[128,2048]{1,0:T(8,128)(2,1)} %param.15) | copy-start | bytes 1572868
  68.2 168.9 %all-gather.8.cloned.1.call-start = ((), (), s32[]{:S(2)}) async-start(), calls=%async_computation.1 | async-start | bytes 8912896 | tf_op jit(solution)/shard_map/all_gather | solution.py:56
  68.9 243.4 %all-gather.10.cloned.1.call-start = ((), (), s32[]{:S(2)}) async-start(), calls=%async_computation.2 | async-start | bytes 8912896 | tf_op jit(solution)/shard_map/all_gather | solution.py:58
  69.5 468.3 %all-gather.12.cloned.1.call-start = ((), (), s32[]{:S(2)}) async-start(), calls=%async_computation.3 | async-start | bytes 35651584 | tf_op jit(solution)/shard_map/all_gather | solution.py:140
  69.7 10.7 %collective-permute-start.1 = (bf16[128,1024]{1,0:T(8,128)(2,1)S(1)}, bf16[128,1024]{1,0:T(8,128)(2,1)S(1)}, u32[]{:S(2)}, u32[]{:S(2)}) collective-permute-start(bf16[128,1024]{1,0:T(8,128)(2,1)S(1)} %get-tuple-element.43), channel_id=1, source_target_pairs={{1,0},{2,1},{3,2},{4,3},{5,4},{6,5},{7,6},{8,7},{9,8},{10,9},{11,1... | collective-permute-start | bytes 786440 | tf_op jit(solution)/shard_map/ppermute | solution.py:24
  71.0 9.4 %collective-permute-start = (bf16[128,1024]{1,0:T(8,128)(2,1)S(1)}, bf16[128,1024]{1,0:T(8,128)(2,1)S(1)}, u32[]{:S(2)}, u32[]{:S(2)}) collective-permute-start(bf16[128,1024]{1,0:T(8,128)(2,1)S(1)} %get-tuple-element.38), channel_id=1, source_target_pairs={{0,1},{1,2},{2,3},{3,4},{4,5},{5,6},{6,7},{7,8},{8,9},{9,10},{10,1... | collective-permute-start | bytes 786440 | tf_op jit(solution)/shard_map/ppermute | solution.py:22
  162.4 74.6 %copy-start = (bf16[128,2048]{1,0:T(8,128)(2,1)S(1)}, bf16[128,2048]{1,0:T(8,128)(2,1)}, u32[]{:S(2)}) copy-start(bf16[128,2048]{1,0:T(8,128)(2,1)} %param.10) | copy-start | bytes 1572868
  165.1 156.7 %copy-start.2 = (bf16[2,512,512]{1,2,0:T(8,128)(2,1)}, bf16[2,512,512]{1,2,0:T(8,128)(2,1)S(1)}, u32[]{:S(2)}) copy-start(bf16[2,512,512]{1,2,0:T(8,128)(2,1)S(1)} %get-tuple-element.35) | copy-start | bytes 3145732
  385.7 1.4 copy-start.4
  417.4 6.6 %copy-start.6 = (bf16[256,2048]{1,0:T(8,128)(2,1)S(1)}, bf16[256,2048]{1,0:T(8,128)(2,1)}, u32[]{:S(2)}) copy-start(bf16[256,2048]{1,0:T(8,128)(2,1)} %reshape.289) | copy-start | bytes 3145732
  419.1 12.9 %collective-permute-start.3 = (bf16[128,1024]{1,0:T(8,128)(2,1)S(1)}, bf16[128,1024]{1,0:T(8,128)(2,1)S(1)}, u32[]{:S(2)}, u32[]{:S(2)}) collective-permute-start(bf16[128,1024]{1,0:T(8,128)(2,1)S(1)} %get-tuple-element.37), channel_id=1, source_target_pairs={{1,0},{2,1},{3,2},{4,3},{5,4},{6,5},{7,6},{8,7},{9,8},{10,9},{11,1... | collective-permute-start | bytes 786440 | tf_op jit(solution)/shard_map/ppermute | solution.py:24
  420.4 10.6 %copy-start.3 = (f32[128,2048]{1,0:T(8,128)S(1)}, f32[128,2048]{1,0:T(8,128)}, u32[]{:S(2)}) copy-start(f32[128,2048]{1,0:T(8,128)} %rev.13) | copy-start | bytes 3145732
  420.4 10.6 %copy-start.5 = (f32[256,2048]{1,0:T(8,128)S(1)}, f32[256,2048]{1,0:T(8,128)}, u32[]{:S(2)}) copy-start(f32[256,2048]{1,0:T(8,128)} %copy-done.4) | copy-start | bytes 6291460
  420.4 11.6 %collective-permute-start.2 = (bf16[128,1024]{1,0:T(8,128)(2,1)S(1)}, bf16[128,1024]{1,0:T(8,128)(2,1)S(1)}, u32[]{:S(2)}, u32[]{:S(2)}) collective-permute-start(bf16[128,1024]{1,0:T(8,128)(2,1)S(1)} %get-tuple-element.36), channel_id=1, source_target_pairs={{0,1},{1,2},{2,3},{3,4},{4,5},{5,6},{6,7},{7,8},{8,9},{9,10},{10,1... | collective-permute-start | bytes 786440 | tf_op jit(solution)/shard_map/ppermute | solution.py:22
  550.0 2.5 copy-start.1
Sparse Core Ops, SparseCore 0:
  10.2 53.2 all-gather.5
  68.3 92.2 all-reduce.4
  162.8 74.2 all-gather.7
  239.1 73.1 all-gather.9
  368.7 169.1 all-gather.11
